TPU v7x, 32 devices: a whole 2x2x4 slice. The times are simulated.
32 devices in a mesh: expert: 8 (over y, x, core), tensor: 4 (over z).
Axes of the slice: x: 2, y: 2, z: 4, core: 2. Of those that a mesh axis runs over, the one named last changes fastest.
Arguments:
- grad_out: bfloat16 [1024, 4096], P('expert', 'tensor'), may hold values from -6 to 6
- expert_ids: int32 [1024, 4], P('expert'), may hold values from 0 to 7, all different within a row
- gate_probs: float32 [1024, 4], P('expert'), may hold values from 0.05 to 0.6
- live: int32 [1024], P('expert'), may hold values 0 or 1
- w_gate: bfloat16 [8, 5376, 4096], P('expert', 'tensor'), may hold values from -0.09375 to 0.09375
- w_up: bfloat16 [8, 5376, 4096], P('expert', 'tensor'), may hold values from -0.09375 to 0.09375
- w_down: bfloat16 [8, 5376, 4096], P('expert', 'tensor'), may hold values from -0.078125 to 0.078125
- saved: bfloat16 [8, 2, 5376, 512], P('expert', None, 'tensor'), may hold values from -8 to 8
Outputs:
- grad_in: bfloat16 [1024, 4096], P('expert', 'tensor')
Inputs may be any that keep to these rules, and one draw needn't show every extreme that they name: `expert_ids`: the 4 ids of a token are different.
All inputs are finite; a program needn't handle non-finite values. No bound on the sum of `live` on one device may be relied on, other than what follows from the above.
Results may differ from a plain program's by a relative error of at most 0.012.
Values may be sent and summed in bfloat16 or wider, within the bound.
A program may use at most 128 MiB of HBM per device.

v0:
```python
import functools

import jax
import jax.numpy as jnp
from jax import lax
from jax.experimental import pallas as pl
from jax.experimental.pallas import tpu as pltpu
from jax.sharding import PartitionSpec as P

MESH = pl.DeviceIdType.MESH
NT = (((1,), (1,)), ((), ()))
NN = (((1,), (0,)), ((), ()))


def dot(a, b, dims):
    return lax.dot_general(a, b, dims, preferred_element_type=jnp.float32)


def mate(me, step, size, sign):
    if size & (size - 1):
        return lax.rem(me + (sign * step) % size, size)
    out, bit = 0, 1
    while bit < size:
        mine = lax.rem(lax.div(me, bit), 2)
        out = out + (1 - mine if step & bit else mine) * bit
        bit *= 2
    return out


def kernel(
    ne, nt, cap, raw0, ids, gates, live, w_gate, w_up, w_down, saved, out,
    wd, wg, wu, sv, svt, dh, sel, gs, back, outgoing, recv, orecv, raw, part, zrecv,
    w_sem, sv_sem, in_send, in_recv, out_send, out_recv, z_send, z_recv, p_send, p_recv,
):
    me = lax.axis_index("expert")
    mz = lax.axis_index("tensor")
    tokens, chunk = raw0.shape
    slots = ne * cap
    hidden = saved.shape[2]
    tops = ids.shape[0]
    steps = range(nt)
    owner = [mate(mz, s, nt, 1) for s in steps]
    zpeer = [mate(mz, s, nt, -1) for s in steps]
    order = sorted(range(1, ne), key=lambda j: (-(j // 2) if j > 1 else 1, j))
    epeer = [mate(me, j, ne, 1) for j in order]

    barrier = pltpu.get_barrier_semaphore()
    for peer in epeer:
        pl.semaphore_signal(barrier, inc=1, device_id=(peer, mz), device_id_type=MESH)
    for s in range(1, nt):
        pl.semaphore_signal(barrier, inc=1, device_id=(me, zpeer[s]), device_id_type=MESH)

    def weight_copy(i, s):
        src = (w_down, w_gate, w_up)[i]
        dst = (wd, wg, wu)[i]
        columns = pl.ds(pl.multiple_of(owner[s] * chunk, chunk), chunk)
        return pltpu.make_async_copy(src.at[0, :, columns], dst.at[s], w_sem.at[i, s])

    saved_copy = pltpu.make_async_copy(saved.at[0], sv, sv_sem.at[0])

    experts = lax.broadcasted_iota(jnp.int32, (ne, tokens), 0)
    alive = live[...] != 0
    chosen = jnp.zeros((ne, tokens), jnp.float32)
    weight = jnp.zeros((ne, tokens), jnp.float32)
    for k in range(tops):
        match = (ids[k : k + 1, :] == experts) & alive
        chosen = chosen + jnp.where(match, 1.0, 0.0)
        weight = weight + jnp.where(match, gates[k : k + 1, :], 0.0)
    row = lax.broadcasted_iota(jnp.int32, (tokens, tokens), 0)
    col = lax.broadcasted_iota(jnp.int32, (tokens, tokens), 1)
    before = jnp.where(row < col, 1.0, 0.0).astype(jnp.bfloat16)
    position = dot(chosen.astype(jnp.bfloat16), before, NN)
    position = jnp.where((chosen > 0.0) & (position < cap), position, -1.0)
    slot = lax.broadcasted_iota(jnp.int32, (cap, tokens), 0).astype(jnp.float32)
    for e in range(ne):
        hit = slot == position[e : e + 1, :]
        sel[e * cap : (e + 1) * cap, :] = jnp.where(hit, 1.0, 0.0).astype(jnp.bfloat16)
        gate = jnp.sum(jnp.where(hit, weight[e : e + 1, :], 0.0), axis=1, keepdims=True)
        gs[e * cap : (e + 1) * cap, :] = jnp.broadcast_to(gate, (cap, gs.shape[1]))

    tile = min(256, chunk)

    def build(src, s):
        @pl.loop(0, chunk // tile)
        def _(c):
            columns = pl.ds(pl.multiple_of(c * tile, tile), tile)
            picked = dot(sel[...], src[:, columns], NN)
            outgoing[s, :, columns] = (gs[:, :1] * picked).astype(jnp.bfloat16)

    def rows(e):
        return pl.ds(pl.multiple_of(e * cap, cap), cap)

    def exchange(s, dst, send, receive):
        for peer in epeer:
            pltpu.make_async_remote_copy(
                src_ref=outgoing.at[s, rows(peer)],
                dst_ref=dst.at[s, rows(me)],
                send_sem=send.at[s],
                recv_sem=receive.at[s],
                device_id=(peer, mz),
                device_id_type=MESH,
            ).start()
        pltpu.make_async_copy(
            outgoing.at[s, rows(me)], dst.at[s, rows(me)], receive.at[s]
        ).start()

    def wait_all(ref, sem):
        pltpu.make_async_copy(ref, ref, sem).wait()

    def z_copy(src, dst, s, send, receive, peer):
        return pltpu.make_async_remote_copy(
            src_ref=src,
            dst_ref=dst,
            send_sem=send.at[s],
            recv_sem=receive.at[s],
            device_id=(me, peer),
            device_id_type=MESH,
        )

    build(raw0, 0)
    pl.semaphore_wait(barrier, ne - 1 + nt - 1)
    z_copies = [
        z_copy(raw0, raw.at[s], s, z_send, z_recv, zpeer[s]) for s in range(1, nt)
    ]
    for copy in z_copies:
        copy.start()
    exchange(0, recv, in_send, in_recv)

    saved_copy.start()
    for s in steps:
        weight_copy(0, s).start()
    for s in reversed(steps):
        weight_copy(1, s).start()
        weight_copy(2, s).start()

    for s in range(1, nt):
        z_copies[s - 1].wait_recv()
        build(raw.at[s], s)
        exchange(s, recv, in_send, in_recv)

    row = lax.broadcasted_iota(jnp.int32, (tokens, tokens), 0)
    col = lax.broadcasted_iota(jnp.int32, (tokens, tokens), 1)
    eye = jnp.where(row == col, 1.0, 0.0).astype(jnp.bfloat16)
    back[...] = dot(eye, sel[...], NT).astype(jnp.bfloat16)
    block = min(128, slots)
    saved_copy.wait()

    @pl.loop(0, slots // block)
    def _(b):
        at = pl.ds(pl.multiple_of(b * block, block), block)
        r = lax.broadcasted_iota(jnp.int32, (block, block), 0)
        c = lax.broadcasted_iota(jnp.int32, (block, block), 1)
        one = jnp.where(r == c, 1.0, 0.0).astype(jnp.bfloat16)
        for i in range(2):
            svt[i, at, :] = dot(one, sv[i, :, at], NT).astype(jnp.bfloat16)

    half = min(256, slots)
    for s in steps:
        weight_copy(0, s).wait()
        wait_all(recv.at[s], in_recv.at[s])

        @pl.loop(0, slots // half)
        def _(b):
            at = pl.ds(pl.multiple_of(b * half, half), half)
            part_sum = dot(recv[s, at, :], wd[s], NT)
            if s == 0:
                dh[at, :] = part_sum
            else:
                dh[at, :] = dh[at, :] + part_sum

    few = 16

    @pl.loop(0, slots // few)
    def _(b):
        at = pl.ds(pl.multiple_of(b * few, few), few)
        grad = dh[at, :]
        a = svt[0, at, :].astype(jnp.float32)
        u = svt[1, at, :].astype(jnp.float32)
        sig = jax.nn.sigmoid(a)
        svt[1, at, :] = (grad * a * sig).astype(jnp.bfloat16)
        svt[0, at, :] = (grad * u * sig * (1.0 + a * (1.0 - sig))).astype(jnp.bfloat16)

    def combine(s, columns):
        return dot(back[...], orecv[s, :, columns], NN)

    p_copies = {
        s: z_copy(part.at[s], zrecv.at[s], s, p_send, p_recv, owner[s])
        for s in range(1, nt)
    }

    def finish(s):
        wait_all(orecv.at[s], out_recv.at[s])
        if s == 0:
            for q in range(1, nt):
                p_copies[q].wait_recv()

        @pl.loop(0, chunk // tile)
        def _(c):
            columns = pl.ds(pl.multiple_of(c * tile, tile), tile)
            total = combine(s, columns)
            if s == 0:
                for q in range(1, nt):
                    total = total + zrecv[q, :, columns].astype(jnp.float32)
                out[:, columns] = total.astype(jnp.bfloat16)
            else:
                part[s, :, columns] = total.astype(jnp.bfloat16)

        if s > 0:
            p_copies[s].start()

    others = outgoing.at[0, pl.ds(0, (ne - 1) * cap)]
    for s in reversed(steps):
        wait_all(others, in_send.at[s])
        weight_copy(1, s).wait()
        weight_copy(2, s).wait()

        @pl.loop(0, chunk // tile)
        def _(c):
            columns = pl.ds(pl.multiple_of(c * tile, tile), tile)
            term = dot(svt[0], wg[s, :, columns], NN)
            term = term + dot(svt[1], wu[s, :, columns], NN)
            outgoing[s, :, columns] = term.astype(jnp.bfloat16)

        exchange(s, orecv, out_send, out_recv)
    for s in reversed(steps):
        finish(s)

    for s in steps:
        wait_all(others, out_send.at[s])
    for s in range(1, nt):
        z_copies[s - 1].wait_send()
        p_copies[s].wait_send()


def shards(grad_out, expert_ids, gate_probs, live, w_gate, w_up, w_down, saved):
    ne = lax.axis_size("expert")
    nt = lax.axis_size("tensor")
    tokens, chunk = grad_out.shape
    cap = tokens * expert_ids.shape[1] // ne
    slots = ne * cap
    hidden = saved.shape[2]
    bf16, f32 = jnp.bfloat16, jnp.float32
    vmem = pl.BlockSpec(memory_space=pltpu.VMEM)
    anywhere = pl.BlockSpec(memory_space=pl.ANY)
    dma = pltpu.SemaphoreType.DMA
    return pl.pallas_call(
        functools.partial(kernel, ne, nt, cap),
        out_shape=jax.ShapeDtypeStruct((tokens, chunk), bf16),
        in_specs=[vmem] * 4 + [anywhere] * 4,
        out_specs=vmem,
        scratch_shapes=[
            pltpu.VMEM((nt, hidden, chunk), bf16),
            pltpu.VMEM((nt, hidden, chunk), bf16),
            pltpu.VMEM((nt, hidden, chunk), bf16),
            pltpu.VMEM((2, hidden, slots), bf16),
            pltpu.VMEM((2, slots, hidden), bf16),
            pltpu.VMEM((slots, hidden), f32),
            pltpu.VMEM((slots, tokens), bf16),
            pltpu.VMEM((slots, 128), f32),
            pltpu.VMEM((tokens, slots), bf16),
            pltpu.VMEM((nt, slots, chunk), bf16),
            pltpu.VMEM((nt, slots, chunk), bf16),
            pltpu.VMEM((nt, slots, chunk), bf16),
            pltpu.VMEM((nt, tokens, chunk), bf16),
            pltpu.VMEM((nt, tokens, chunk), bf16),
            pltpu.VMEM((nt, tokens, chunk), bf16),
            dma((3, nt)),
            dma((1,)),
            dma((nt,)),
            dma((nt,)),
            dma((nt,)),
            dma((nt,)),
            dma((nt,)),
            dma((nt,)),
            dma((nt,)),
            dma((nt,)),
        ],
        compiler_params=pltpu.CompilerParams(
            collective_id=0, has_side_effects=True, vmem_limit_bytes=67043328
        ),
    )(
        grad_out,
        expert_ids.T,
        gate_probs.T,
        live.reshape(1, tokens),
        w_gate,
        w_up,
        w_down,
        saved,
    )


def solution(mesh):
    placed = (
        P("expert", "tensor"),
        P("expert", None),
        P("expert", None),
        P("expert"),
        P("expert", "tensor", None),
        P("expert", "tensor", None),
        P("expert", "tensor", None),
        P("expert", None, "tensor", None),
    )
    return jax.shard_map(
        shards, mesh=mesh, in_specs=placed, out_specs=P("expert", "tensor"), check_vma=False
    )
```

profile of v0, /device:TPU:0, one launch (start us, length us, event | category | flops | bytes accessed | tf_op | source)
XLA Modules:
  0.0 113.1 jit_solution(11197897355123632137)
XLA Ops:
  0.0 111.4 %shard_map.82 = bf16[128,1024]{1,0:T(8,128)(2,1)} custom-call(bf16[128,1024]{1,0:T(8,128)(2,1)} %raw0.1, s32[4,128]{1,0:T(4,128)} %bitcast.3, f32[4,128]{1,0:T(4,128)} %bitcast.4, s32[1,128]{1,0:T(1,128)} %bitcast.5, bf16[1,1344,4096]{2,1,0:T(8,128)(2,1)} %w_gate.1, bf16[1,1344,4096]{2,1,0:T(8,128)(2,1)} %w_up.1, bf16[1,1344,4096]{2,1,0:T(8,128)(2,1)} %w_down.1, ...), custom_call_target="tpu_custom_call" | custom-call | tf_op jit(solution)/shard_map/pallas_call | solution.py:246
  111.4 1.7 %copy.10 = bf16[128,1024]{1,0:T(8,128)(2,1)} copy(bf16[128,1024]{1,0:T(8,128)(2,1)} %shard_map.82) | data formatting | bytes 524288
where the time goes:
time: 113 us
  Pallas kernels  111 us (98%)
  local copies, waits for them, and re-layouts  1.67 us (1%)
    pallas_call x1, Pallas kernels, shards(): pl.pallas_call(functools.partial(kernel, ne, nt, cap), out_shape=jax.Shap...  111 us

commit v1 on v0

--- a/solution.py
+++ b/solution.py
@@ -27,10 +27,19 @@
     return out
 
 
+def shortcuts(nt, pieces):
+    ahead = [0] * nt
+    for s, share in ((1, 2), (2, 4)):
+        if s < nt:
+            ahead[s] = pieces // share
+    return ahead
+
+
 def kernel(
     ne, nt, cap, raw0, ids, gates, live, w_gate, w_up, w_down, saved, out,
-    wd, wg, wu, sv, svt, dh, sel, gs, back, outgoing, recv, orecv, raw, part, zrecv,
+    wd, wg, wu, sv, svt, dh, sel, gs, back, outgoing, recv, orecv, raw, part, zrecv, zterm,
     w_sem, sv_sem, in_send, in_recv, out_send, out_recv, z_send, z_recv, p_send, p_recv,
+    b_send, t_send, t_recv,
 ):
     me = lax.axis_index("expert")
     mz = lax.axis_index("tensor")
@@ -79,52 +88,69 @@
         gs[e * cap : (e + 1) * cap, :] = jnp.broadcast_to(gate, (cap, gs.shape[1]))
 
     tile = min(256, chunk)
-
-    def build(src, s):
-        @pl.loop(0, chunk // tile)
-        def _(c):
-            columns = pl.ds(pl.multiple_of(c * tile, tile), tile)
-            picked = dot(sel[...], src[:, columns], NN)
-            outgoing[s, :, columns] = (gs[:, :1] * picked).astype(jnp.bfloat16)
+    pieces = chunk // tile
+    ahead = shortcuts(nt, pieces)
+    crossing = [(s, j) for s in steps for j in range(ahead[s])]
+
+    def piece(j):
+        return pl.ds(pl.multiple_of(j * tile, tile), tile)
+
+    def build(src, s, j):
+        picked = dot(sel[...], src[:, piece(j)], NN)
+        outgoing[s, :, piece(j)] = (gs[:, :1] * picked).astype(jnp.bfloat16)
 
     def rows(e):
         return pl.ds(pl.multiple_of(e * cap, cap), cap)
 
-    def exchange(s, dst, send, receive):
+    def exchange(s, j, dst, send, receive):
         for peer in epeer:
             pltpu.make_async_remote_copy(
-                src_ref=outgoing.at[s, rows(peer)],
-                dst_ref=dst.at[s, rows(me)],
-                send_sem=send.at[s],
-                recv_sem=receive.at[s],
+                src_ref=outgoing.at[s, rows(peer), piece(j)],
+                dst_ref=dst.at[s, rows(me), piece(j)],
+                send_sem=send.at[s, j],
+                recv_sem=receive.at[s, j],
                 device_id=(peer, mz),
                 device_id_type=MESH,
             ).start()
         pltpu.make_async_copy(
-            outgoing.at[s, rows(me)], dst.at[s, rows(me)], receive.at[s]
+            outgoing.at[s, rows(me), piece(j)],
+            dst.at[s, rows(me), piece(j)],
+            receive.at[s, j],
         ).start()
 
     def wait_all(ref, sem):
         pltpu.make_async_copy(ref, ref, sem).wait()
 
-    def z_copy(src, dst, s, send, receive, peer):
+    def z_copy(src, dst, send, receive, peer):
         return pltpu.make_async_remote_copy(
             src_ref=src,
             dst_ref=dst,
-            send_sem=send.at[s],
-            recv_sem=receive.at[s],
+            send_sem=send,
+            recv_sem=receive,
             device_id=(me, peer),
             device_id_type=MESH,
         )
 
-    build(raw0, 0)
+    def beyond(s):
+        return pl.ds(ahead[s] * tile, chunk - ahead[s] * tile)
+
     pl.semaphore_wait(barrier, ne - 1 + nt - 1)
-    z_copies = [
-        z_copy(raw0, raw.at[s], s, z_send, z_recv, zpeer[s]) for s in range(1, nt)
-    ]
-    for copy in z_copies:
+    z_copies = {
+        s: z_copy(
+            raw0.at[:, beyond(s)], raw.at[s, :, beyond(s)], z_send.at[s], z_recv.at[s], zpeer[s]
+        )
+        for s in range(1, nt)
+    }
+    for copy in z_copies.values():
         copy.start()
-    exchange(0, recv, in_send, in_recv)
+
+    def give(src, s):
+        @pl.loop(ahead[s], pieces)
+        def _(j):
+            build(src, s, j)
+            exchange(s, j, recv, in_send, in_recv)
+
+    give(raw0, 0)
 
     saved_copy.start()
     for s in steps:
@@ -133,10 +159,21 @@
         weight_copy(1, s).start()
         weight_copy(2, s).start()
 
+    shared = {
+        (s, j): z_copy(
+            recv.at[0, :, piece(j)], recv.at[s, :, piece(j)], b_send.at[k], in_recv.at[s, j], zpeer[s]
+        )
+        for k, (s, j) in enumerate(crossing)
+    }
     for s in range(1, nt):
-        z_copies[s - 1].wait_recv()
-        build(raw.at[s], s)
-        exchange(s, recv, in_send, in_recv)
+        z_copies[s].wait_recv()
+        give(raw.at[s], s)
+        if s == 1:
+            for j in range(max(ahead)):
+                wait_all(recv.at[0, :, piece(j)], in_recv.at[0, j])
+                for q in range(1, nt):
+                    if j < ahead[q]:
+                        shared[q, j].start()
 
     row = lax.broadcasted_iota(jnp.int32, (tokens, tokens), 0)
     col = lax.broadcasted_iota(jnp.int32, (tokens, tokens), 1)
@@ -157,7 +194,8 @@
     half = min(256, slots)
     for s in steps:
         weight_copy(0, s).wait()
-        wait_all(recv.at[s], in_recv.at[s])
+        for j in range(0 if s > 0 or nt == 1 else max(ahead), pieces):
+            wait_all(recv.at[s, :, piece(j)], in_recv.at[s, j])
 
         @pl.loop(0, slots // half)
         def _(b):
@@ -180,56 +218,97 @@
         svt[1, at, :] = (grad * a * sig).astype(jnp.bfloat16)
         svt[0, at, :] = (grad * u * sig * (1.0 + a * (1.0 - sig))).astype(jnp.bfloat16)
 
-    def combine(s, columns):
-        return dot(back[...], orecv[s, :, columns], NN)
+    def combine(s, j):
+        return dot(back[...], orecv[s, :, piece(j)], NN)
 
     p_copies = {
-        s: z_copy(part.at[s], zrecv.at[s], s, p_send, p_recv, owner[s])
+        s: z_copy(
+            part.at[s, :, beyond(s)], zrecv.at[s, :, beyond(s)], p_send.at[s], p_recv.at[s], owner[s]
+        )
         for s in range(1, nt)
     }
-
-    def finish(s):
-        wait_all(orecv.at[s], out_recv.at[s])
-        if s == 0:
-            for q in range(1, nt):
-                p_copies[q].wait_recv()
-
-        @pl.loop(0, chunk // tile)
-        def _(c):
-            columns = pl.ds(pl.multiple_of(c * tile, tile), tile)
-            total = combine(s, columns)
-            if s == 0:
-                for q in range(1, nt):
-                    total = total + zrecv[q, :, columns].astype(jnp.float32)
-                out[:, columns] = total.astype(jnp.bfloat16)
-            else:
-                part[s, :, columns] = total.astype(jnp.bfloat16)
-
-        if s > 0:
-            p_copies[s].start()
-
-    others = outgoing.at[0, pl.ds(0, (ne - 1) * cap)]
-    for s in reversed(steps):
-        wait_all(others, in_send.at[s])
+    t_copies = {
+        (s, j): z_copy(
+            outgoing.at[s, :, piece(j)], zterm.at[k], t_send.at[k], t_recv.at[k], owner[s]
+        )
+        for k, (s, j) in enumerate(crossing)
+    }
+    others = outgoing.at[0, pl.ds(0, (ne - 1) * cap), pl.ds(0, tile)]
+
+    def term(s, j):
+        total = dot(svt[0], wg[s, :, piece(j)], NN)
+        return total + dot(svt[1], wu[s, :, piece(j)], NN)
+
+    def hand(s, low, high):
+        @pl.loop(low, high)
+        def _(j):
+            wait_all(others, in_send.at[s, j])
+            outgoing[s, :, piece(j)] = term(s, j).astype(jnp.bfloat16)
+            exchange(s, j, orecv, out_send, out_recv)
+
+    def hand_across(s):
+        for j in range(ahead[s]):
+            outgoing[s, :, piece(j)] = term(s, j).astype(jnp.bfloat16)
+            t_copies[s, j].start()
+
+    def weights_of(s):
         weight_copy(1, s).wait()
         weight_copy(2, s).wait()
 
-        @pl.loop(0, chunk // tile)
-        def _(c):
-            columns = pl.ds(pl.multiple_of(c * tile, tile), tile)
-            term = dot(svt[0], wg[s, :, columns], NN)
-            term = term + dot(svt[1], wu[s, :, columns], NN)
-            outgoing[s, :, columns] = term.astype(jnp.bfloat16)
-
-        exchange(s, orecv, out_send, out_recv)
-    for s in reversed(steps):
-        finish(s)
+    last = nt - 1
+    lead = ahead[last] if last == 0 else min(ahead[last] + 1, pieces)
+    if last > 0:
+        weights_of(last)
+        hand(last, ahead[last], lead)
+        for s in range(1, nt):
+            if ahead[s] > 0:
+                if s < last:
+                    weights_of(s)
+                hand_across(s)
+        hand(last, lead, pieces)
+    for s in reversed(range(1, last)):
+        if ahead[s] == 0:
+            weights_of(s)
+        hand(s, ahead[s], pieces)
+    weights_of(0)
+    hand(0, max(ahead), pieces)
+    for j in reversed(range(max(ahead))):
+        total = term(0, j)
+        for k, (s, q) in enumerate(crossing):
+            if q == j:
+                t_copies[s, q].wait_recv()
+                total = total + zterm[k].astype(jnp.float32)
+        wait_all(others, in_send.at[0, j])
+        outgoing[0, :, piece(j)] = total.astype(jnp.bfloat16)
+        exchange(0, j, orecv, out_send, out_recv)
+
+    for s in reversed(range(1, nt)):
+
+        @pl.loop(ahead[s], pieces)
+        def _(j):
+            wait_all(orecv.at[s, :, piece(j)], out_recv.at[s, j])
+            part[s, :, piece(j)] = combine(s, j).astype(jnp.bfloat16)
+
+        p_copies[s].start()
+    for s in range(1, nt):
+        p_copies[s].wait_recv()
+    for j in [*range(max(ahead), pieces), *reversed(range(max(ahead)))]:
+        wait_all(orecv.at[0, :, piece(j)], out_recv.at[0, j])
+        total = combine(0, j)
+        for q in range(1, nt):
+            if j >= ahead[q]:
+                total = total + zrecv[q, :, piece(j)].astype(jnp.float32)
+        out[:, piece(j)] = total.astype(jnp.bfloat16)
 
     for s in steps:
-        wait_all(others, out_send.at[s])
+        for j in range(ahead[s], pieces):
+            wait_all(others, out_send.at[s, j])
     for s in range(1, nt):
-        z_copies[s - 1].wait_send()
+        z_copies[s].wait_send()
         p_copies[s].wait_send()
+    for pair in crossing:
+        shared[pair].wait_send()
+        t_copies[pair].wait_send()
 
 
 def shards(grad_out, expert_ids, gate_probs, live, w_gate, w_up, w_down, saved):
@@ -239,6 +318,9 @@
     cap = tokens * expert_ids.shape[1] // ne
     slots = ne * cap
     hidden = saved.shape[2]
+    tile = min(256, chunk)
+    pieces = chunk // tile
+    crossings = max(1, sum(shortcuts(nt, pieces)))
     bf16, f32 = jnp.bfloat16, jnp.float32
     vmem = pl.BlockSpec(memory_space=pltpu.VMEM)
     anywhere = pl.BlockSpec(memory_space=pl.ANY)
@@ -264,16 +346,20 @@
             pltpu.VMEM((nt, tokens, chunk), bf16),
             pltpu.VMEM((nt, tokens, chunk), bf16),
             pltpu.VMEM((nt, tokens, chunk), bf16),
+            pltpu.VMEM((crossings, slots, tile), bf16),
             dma((3, nt)),
             dma((1,)),
+            dma((nt, pieces)),
+            dma((nt, pieces)),
+            dma((nt, pieces)),
+            dma((nt, pieces)),
             dma((nt,)),
             dma((nt,)),
             dma((nt,)),
             dma((nt,)),
-            dma((nt,)),
-            dma((nt,)),
-            dma((nt,)),
-            dma((nt,)),
+            dma((crossings,)),
+            dma((crossings,)),
+            dma((crossings,)),
         ],
         compiler_params=pltpu.CompilerParams(
             collective_id=0, has_side_effects=True, vmem_limit_bytes=67043328

time: 113 us -> 98 us (0.87)
  Pallas kernels: 111 us -> 96.2 us
    pallas_call x1, Pallas kernels: 111 us -> 96.2 us  [shards(): pl.pallas_call(functools.partial(kernel, ne, nt, cap), out_shape=jax.Shap...]
where the time goes in v1:
time: 98 us; the launch traced here: 97.9 us
  Pallas kernels  96.2 us (98%)
  local copies, waits for them, and re-layouts  1.67 us (2%)
    pallas_call x1, Pallas kernels, shards(): pl.pallas_call(functools.partial(kernel, ne, nt, cap), out_shape=jax.Shap...  96.2 us

profile of v1, /device:TPU:0, one launch (start us, length us, event | category | flops | bytes accessed | tf_op | source)
XLA Modules:
  0.0 97.9 jit_solution(5130881456487631840)
XLA Ops:
  0.0 96.2 %shard_map.82 = bf16[128,1024]{1,0:T(8,128)(2,1)} custom-call(bf16[128,1024]{1,0:T(8,128)(2,1)} %raw0.1, s32[4,128]{1,0:T(4,128)} %bitcast.3, f32[4,128]{1,0:T(4,128)} %bitcast.4, s32[1,128]{1,0:T(1,128)} %bitcast.5, bf16[1,1344,4096]{2,1,0:T(8,128)(2,1)} %w_gate.1, bf16[1,1344,4096]{2,1,0:T(8,128)(2,1)} %w_up.1, bf16[1,1344,4096]{2,1,0:T(8,128)(2,1)} %w_down.1, ...), custom_call_target="tpu_custom_call" | custom-call | tf_op jit(solution)/shard_map/pallas_call | solution.py:328
  96.2 1.7 %copy.10 = bf16[128,1024]{1,0:T(8,128)(2,1)} copy(bf16[128,1024]{1,0:T(8,128)(2,1)} %shard_map.82) | data formatting | bytes 524288

commit v2 on v0

v2 whole, which is shorter than its diff:
```python
import functools

import jax
import jax.numpy as jnp
from jax import lax
from jax.experimental import pallas as pl
from jax.experimental.pallas import tpu as pltpu
from jax.sharding import PartitionSpec as P

MESH = pl.DeviceIdType.MESH
NT = (((1,), (1,)), ((), ()))
NN = (((1,), (0,)), ((), ()))


def dot(a, b, dims):
    return lax.dot_general(a, b, dims, preferred_element_type=jnp.float32)


def mate(me, step, size, sign):
    if size & (size - 1):
        return lax.rem(me + (sign * step) % size, size)
    out, bit = 0, 1
    while bit < size:
        mine = lax.rem(lax.div(me, bit), 2)
        out = out + (1 - mine if step & bit else mine) * bit
        bit *= 2
    return out


INWARD = ((1, 2), (2, 1))
OUTWARD = ((1, 2), (2, 1))


def shortcuts(nt, pieces, shares):
    across = [0] * nt
    for s, quarters in shares:
        if s < nt:
            across[s] = pieces * quarters // 4
    return across


def kernel(
    ne, nt, cap, raw0, ids, gates, live, w_gate, w_up, w_down, saved, out,
    wd, wg, wu, sv, svt, dh, sel, gs, back, outgoing, recv, orecv, raw, part, zrecv, zterm,
    w_sem, sv_sem, in_send, in_recv, out_send, out_recv, z_send, z_recv, p_send, p_recv,
    b_send, t_send, t_recv,
):
    me = lax.axis_index("expert")
    mz = lax.axis_index("tensor")
    tokens, chunk = raw0.shape
    slots = ne * cap
    hidden = saved.shape[2]
    tops = ids.shape[0]
    steps = range(nt)
    owner = [mate(mz, s, nt, 1) for s in steps]
    zpeer = [mate(mz, s, nt, -1) for s in steps]
    order = sorted(range(1, ne), key=lambda j: (-(j // 2) if j > 1 else 1, j))
    epeer = [mate(me, j, ne, 1) for j in order]

    barrier = pltpu.get_barrier_semaphore()
    for peer in epeer:
        pl.semaphore_signal(barrier, inc=1, device_id=(peer, mz), device_id_type=MESH)
    for s in range(1, nt):
        pl.semaphore_signal(barrier, inc=1, device_id=(me, zpeer[s]), device_id_type=MESH)

    def weight_copy(i, s):
        src = (w_down, w_gate, w_up)[i]
        dst = (wd, wg, wu)[i]
        columns = pl.ds(pl.multiple_of(owner[s] * chunk, chunk), chunk)
        return pltpu.make_async_copy(src.at[0, :, columns], dst.at[s], w_sem.at[i, s])

    saved_copy = pltpu.make_async_copy(saved.at[0], sv, sv_sem.at[0])

    tile = min(256, chunk)
    pieces = chunk // tile
    ahead = shortcuts(nt, pieces, INWARD)
    astern = shortcuts(nt, pieces, OUTWARD)
    halves = range(2)
    part_cap, part_slots = cap // 2, slots // 2

    def crossings(across):
        return [(s, j, h) for h in halves for j in range(max(across)) for s in steps if j < across[s]]

    def span(h):
        return pl.ds(h * part_slots, part_slots)

    def piece(j):
        return pl.ds(pl.multiple_of(j * tile, tile), tile)

    def build(src, s, j, h):
        picked = dot(sel[span(h), :], src[:, piece(j)], NN)
        outgoing[s, span(h), piece(j)] = (gs[span(h), :1] * picked).astype(jnp.bfloat16)

    def rows(h, e):
        return pl.ds(pl.multiple_of(h * part_slots + e * part_cap, part_cap), part_cap)

    def exchange(s, j, h, dst, send, receive):
        for peer in epeer:
            pltpu.make_async_remote_copy(
                src_ref=outgoing.at[s, rows(h, peer), piece(j)],
                dst_ref=dst.at[s, rows(h, me), piece(j)],
                send_sem=send.at[s, j, h],
                recv_sem=receive.at[s, j, h],
                device_id=(peer, mz),
                device_id_type=MESH,
            ).start()
        pltpu.make_async_copy(
            outgoing.at[s, rows(h, me), piece(j)],
            dst.at[s, rows(h, me), piece(j)],
            receive.at[s, j, h],
        ).start()

    def wait_all(ref, sem):
        pltpu.make_async_copy(ref, ref, sem).wait()

    def z_copy(src, dst, send, receive, peer):
        return pltpu.make_async_remote_copy(
            src_ref=src,
            dst_ref=dst,
            send_sem=send,
            recv_sem=receive,
            device_id=(me, peer),
            device_id_type=MESH,
        )

    def beyond(s, across):
        return pl.ds(across[s] * tile, chunk - across[s] * tile)

    pl.semaphore_wait(barrier, ne - 1 + nt - 1)
    z_copies = {
        s: z_copy(
            raw0.at[:, beyond(s, ahead)],
            raw.at[s, :, beyond(s, ahead)],
            z_send.at[s],
            z_recv.at[s],
            zpeer[s],
        )
        for s in range(1, nt)
    }
    for copy in z_copies.values():
        copy.start()

    experts = lax.broadcasted_iota(jnp.int32, (ne, tokens), 0)
    alive = live[...] != 0
    chosen = jnp.zeros((ne, tokens), jnp.float32)
    weight = jnp.zeros((ne, tokens), jnp.float32)
    for k in range(tops):
        match = (ids[k : k + 1, :] == experts) & alive
        chosen = chosen + jnp.where(match, 1.0, 0.0)
        weight = weight + jnp.where(match, gates[k : k + 1, :], 0.0)
    row = lax.broadcasted_iota(jnp.int32, (tokens, tokens), 0)
    col = lax.broadcasted_iota(jnp.int32, (tokens, tokens), 1)
    before = jnp.where(row < col, 1.0, 0.0).astype(jnp.bfloat16)
    position = dot(chosen.astype(jnp.bfloat16), before, NN)
    position = jnp.where((chosen > 0.0) & (position < cap), position, -1.0)
    slot = lax.broadcasted_iota(jnp.int32, (cap, tokens), 0).astype(jnp.float32)
    for e in range(ne):
        hit = slot == position[e : e + 1, :]
        gate = jnp.sum(jnp.where(hit, weight[e : e + 1, :], 0.0), axis=1, keepdims=True)
        gate = jnp.broadcast_to(gate, (cap, gs.shape[1]))
        hit = jnp.where(hit, 1.0, 0.0)
        for h in halves:
            some = slice(h * part_cap, (h + 1) * part_cap)
            sel[rows(h, e), :] = hit[some].astype(jnp.bfloat16)
            gs[rows(h, e), :] = gate[some]

    def give(src, s, which):
        @pl.loop(ahead[s], pieces)
        def _(j):
            for h in which:
                build(src, s, j, h)
                exchange(s, j, h, recv, in_send, in_recv)

    give(raw0, 0, halves)

    saved_copy.start()
    for s in steps:
        weight_copy(0, s).start()
    for s in reversed(steps):
        weight_copy(1, s).start()
        weight_copy(2, s).start()

    shared = {
        (s, j, h): z_copy(
            recv.at[0, span(h), piece(j)],
            recv.at[s, span(h), piece(j)],
            b_send.at[k],
            in_recv.at[s, j, h],
            zpeer[s],
        )
        for k, (s, j, h) in enumerate(crossings(ahead))
    }

    def landed(dst, s, j, h, receive):
        wait_all(dst.at[s, span(h), piece(j)], receive.at[s, j, h])

    early = max(1, nt // 2)
    for s in range(1, nt):
        z_copies[s].wait_recv()
        give(raw.at[s], s, halves if s < early else [0])
        if s == 1:
            for h in halves:
                for j in range(max(ahead)):
                    landed(recv, 0, j, h, in_recv)
            for copy in shared.values():
                copy.start()
    for s in range(early, nt):
        give(raw.at[s], s, [1])

    row = lax.broadcasted_iota(jnp.int32, (tokens, tokens), 0)
    col = lax.broadcasted_iota(jnp.int32, (tokens, tokens), 1)
    eye = jnp.where(row == col, 1.0, 0.0).astype(jnp.bfloat16)
    back[...] = dot(eye, sel[...], NT).astype(jnp.bfloat16)
    block = max(cap, min(128, slots))
    saved_copy.wait()

    @pl.loop(0, slots // block)
    def _(b):
        at = pl.ds(pl.multiple_of(b * block, block), block)
        r = lax.broadcasted_iota(jnp.int32, (block, block), 0)
        c = lax.broadcasted_iota(jnp.int32, (block, block), 1)
        one = jnp.where(r == c, 1.0, 0.0).astype(jnp.bfloat16)
        for i in range(2):
            turned = dot(one, sv[i, :, at], NT).astype(jnp.bfloat16)
            for g in range(block // cap):
                for h in halves:
                    some = slice(g * cap + h * part_cap, g * cap + (h + 1) * part_cap)
                    svt[i, rows(h, b * (block // cap) + g), :] = turned[some]

    def contract(s, h):
        for j in range(pieces):
            if s > 0 or nt == 1 or j >= max(ahead):
                landed(recv, s, j, h, in_recv)
        part_sum = dot(recv[s, span(h), :], wd[s], NT)
        dh[span(h), :] = part_sum if s == 0 else dh[span(h), :] + part_sum

    few = 16

    def activate(h):
        @pl.loop(h * part_slots // few, (h + 1) * part_slots // few)
        def _(b):
            at = pl.ds(pl.multiple_of(b * few, few), few)
            grad = dh[at, :]
            a = svt[0, at, :].astype(jnp.float32)
            u = svt[1, at, :].astype(jnp.float32)
            sig = jax.nn.sigmoid(a)
            svt[1, at, :] = (grad * a * sig).astype(jnp.bfloat16)
            svt[0, at, :] = (grad * u * sig * (1.0 + a * (1.0 - sig))).astype(jnp.bfloat16)

    def combine(s, j):
        return dot(back[...], orecv[s, :, piece(j)], NN)

    p_copies = {
        s: z_copy(
            part.at[s, :, beyond(s, astern)],
            zrecv.at[s, :, beyond(s, astern)],
            p_send.at[s],
            p_recv.at[s],
            owner[s],
        )
        for s in range(1, nt)
    }
    t_copies = {
        (s, j, h): z_copy(
            outgoing.at[s, span(h), piece(j)], zterm.at[k], t_send.at[k], t_recv.at[k], owner[s]
        )
        for k, (s, j, h) in enumerate(crossings(astern))
    }
    others = outgoing.at[0, pl.ds(0, (ne - 1) * part_cap), pl.ds(0, tile)]

    def term(s, j, h):
        total = dot(svt[0, span(h), :], wg[s, :, piece(j)], NN)
        return total + dot(svt[1, span(h), :], wu[s, :, piece(j)], NN)

    def vacant(s, j, h):
        wait_all(others, in_send.at[s, j, h])

    def hand(s, h, low, high):
        @pl.loop(low, high)
        def _(j):
            vacant(s, j, h)
            outgoing[s, span(h), piece(j)] = term(s, j, h).astype(jnp.bfloat16)
            exchange(s, j, h, orecv, out_send, out_recv)

    def hand_across(s, h):
        for j in range(astern[s]):
            if j >= ahead[s]:
                vacant(s, j, h)
            outgoing[s, span(h), piece(j)] = term(s, j, h).astype(jnp.bfloat16)
            t_copies[s, j, h].start()

    last = nt - 1

    def send_back_own(h):
        for j in reversed(range(max(astern))):
            total = term(0, j, h)
            for k, (s, q, half) in enumerate(crossings(astern)):
                if q == j and half == h:
                    t_copies[s, q, h].wait_recv()
                    total = total + zterm[k].astype(jnp.float32)
            vacant(0, j, h)
            outgoing[0, span(h), piece(j)] = total.astype(jnp.bfloat16)
            exchange(0, j, h, orecv, out_send, out_recv)

    for s in steps:
        weight_copy(0, s).wait()
        contract(s, 0)
        if s == 0:
            contract(s, 1)
    activate(0)
    for s in steps:
        weight_copy(1, s).wait()
        weight_copy(2, s).wait()
    hand(0, 0, max(astern), pieces)
    for s in range(1, nt):
        hand_across(s, 0)
    for s in [*range(1, early), *([last] if last >= early else [])]:
        hand(s, 0, astern[s], pieces)
    for s in range(1, nt):
        contract(s, 1)
    activate(1)
    for s in reversed(range(early, nt)):
        if s < last:
            hand(s, 0, astern[s], pieces)
        hand(s, 1, astern[s], pieces)
        if s == last:
            for q in range(1, nt):
                hand_across(q, 1)
    for s in reversed(range(1, early)):
        hand(s, 1, astern[s], pieces)
    send_back_own(0)
    hand(0, 1, max(astern), pieces)
    send_back_own(1)

    for s in reversed(range(1, nt)):

        @pl.loop(astern[s], pieces)
        def _(j):
            for h in halves:
                landed(orecv, s, j, h, out_recv)
            part[s, :, piece(j)] = combine(s, j).astype(jnp.bfloat16)

        p_copies[s].start()
    for s in range(1, nt):
        p_copies[s].wait_recv()
    for j in [*range(max(astern), pieces), *reversed(range(max(astern)))]:
        for h in halves:
            landed(orecv, 0, j, h, out_recv)
        total = combine(0, j)
        for q in range(1, nt):
            if j >= astern[q]:
                total = total + zrecv[q, :, piece(j)].astype(jnp.float32)
        out[:, piece(j)] = total.astype(jnp.bfloat16)

    for s in steps:
        for j in range(pieces):
            for h in halves:
                if j >= astern[s]:
                    wait_all(others, out_send.at[s, j, h])
    for s in range(1, nt):
        z_copies[s].wait_send()
        p_copies[s].wait_send()
    for copy in [*shared.values(), *t_copies.values()]:
        copy.wait_send()


def shards(grad_out, expert_ids, gate_probs, live, w_gate, w_up, w_down, saved):
    ne = lax.axis_size("expert")
    nt = lax.axis_size("tensor")
    tokens, chunk = grad_out.shape
    cap = tokens * expert_ids.shape[1] // ne
    slots = ne * cap
    hidden = saved.shape[2]
    tile = min(256, chunk)
    pieces = chunk // tile
    inward = max(1, 2 * sum(shortcuts(nt, pieces, INWARD)))
    outward = max(1, 2 * sum(shortcuts(nt, pieces, OUTWARD)))
    bf16, f32 = jnp.bfloat16, jnp.float32
    vmem = pl.BlockSpec(memory_space=pltpu.VMEM)
    anywhere = pl.BlockSpec(memory_space=pl.ANY)
    dma = pltpu.SemaphoreType.DMA
    return pl.pallas_call(
        functools.partial(kernel, ne, nt, cap),
        out_shape=jax.ShapeDtypeStruct((tokens, chunk), bf16),
        in_specs=[vmem] * 4 + [anywhere] * 4,
        out_specs=vmem,
        scratch_shapes=[
            pltpu.VMEM((nt, hidden, chunk), bf16),
            pltpu.VMEM((nt, hidden, chunk), bf16),
            pltpu.VMEM((nt, hidden, chunk), bf16),
            pltpu.VMEM((2, hidden, slots), bf16),
            pltpu.VMEM((2, slots, hidden), bf16),
            pltpu.VMEM((slots, hidden), f32),
            pltpu.VMEM((slots, tokens), bf16),
            pltpu.VMEM((slots, 128), f32),
            pltpu.VMEM((tokens, slots), bf16),
            pltpu.VMEM((nt, slots, chunk), bf16),
            pltpu.VMEM((nt, slots, chunk), bf16),
            pltpu.VMEM((nt, slots, chunk), bf16),
            pltpu.VMEM((nt, tokens, chunk), bf16),
            pltpu.VMEM((nt, tokens, chunk), bf16),
            pltpu.VMEM((nt, tokens, chunk), bf16),
            pltpu.VMEM((outward, slots // 2, tile), bf16),
            dma((3, nt)),
            dma((1,)),
            dma((nt, pieces, 2)),
            dma((nt, pieces, 2)),
            dma((nt, pieces, 2)),
            dma((nt, pieces, 2)),
            dma((nt,)),
            dma((nt,)),
            dma((nt,)),
            dma((nt,)),
            dma((inward,)),
            dma((outward,)),
            dma((outward,)),
        ],
        compiler_params=pltpu.CompilerParams(
            collective_id=0, has_side_effects=True, vmem_limit_bytes=67043328
        ),
    )(
        grad_out,
        expert_ids.T,
        gate_probs.T,
        live.reshape(1, tokens),
        w_gate,
        w_up,
        w_down,
        saved,
    )


def solution(mesh):
    placed = (
        P("expert", "tensor"),
        P("expert", None),
        P("expert", None),
        P("expert"),
        P("expert", "tensor", None),
        P("expert", "tensor", None),
        P("expert", "tensor", None),
        P("expert", None, "tensor", None),
    )
    return jax.shard_map(
        shards, mesh=mesh, in_specs=placed, out_specs=P("expert", "tensor"), check_vma=False
    )
```

time: 113 us -> 95.7 us (0.85)
  Pallas kernels: 111 us -> 93.9 us
    pallas_call x1, Pallas kernels: 111 us -> 93.9 us  [shards(): pl.pallas_call(functools.partial(kernel, ne, nt, cap), out_shape=jax.Shap...]
where the time goes in v2:
time: 95.7 us; the launch traced here: 95.5 us
  Pallas kernels  93.9 us (98%)
  local copies, waits for them, and re-layouts  1.67 us (2%)
    pallas_call x1, Pallas kernels, shards(): pl.pallas_call(functools.partial(kernel, ne, nt, cap), out_shape=jax.Shap...  93.9 us

profile of v2, /device:TPU:0, one launch (start us, length us, event | category | flops | bytes accessed | tf_op | source)
XLA Modules:
  0.0 95.5 jit_solution(12568276388410266123)
XLA Ops:
  0.0 93.9 %shard_map.82 = bf16[128,1024]{1,0:T(8,128)(2,1)} custom-call(bf16[128,1024]{1,0:T(8,128)(2,1)} %raw0.1, s32[4,128]{1,0:T(4,128)} %bitcast.3, f32[4,128]{1,0:T(4,128)} %bitcast.4, s32[1,128]{1,0:T(1,128)} %bitcast.5, bf16[1,1344,4096]{2,1,0:T(8,128)(2,1)} %w_gate.1, bf16[1,1344,4096]{2,1,0:T(8,128)(2,1)} %w_up.1, bf16[1,1344,4096]{2,1,0:T(8,128)(2,1)} %w_down.1, ...), custom_call_target="tpu_custom_call" | custom-call | tf_op jit(solution)/shard_map/pallas_call | solution.py:382
  93.9 1.7 %copy.10 = bf16[128,1024]{1,0:T(8,128)(2,1)} copy(bf16[128,1024]{1,0:T(8,128)(2,1)} %shard_map.82) | data formatting | bytes 524288

commit v3 on v2

--- a/solution.py
+++ b/solution.py
@@ -79,7 +79,7 @@
     part_cap, part_slots = cap // 2, slots // 2
 
     def crossings(across):
-        return [(s, j, h) for h in halves for j in range(max(across)) for s in steps if j < across[s]]
+        return [(s, j, h) for h in halves for s in steps for j in range(across[s])]
 
     def span(h):
         return pl.ds(h * part_slots, part_slots)
@@ -276,11 +276,15 @@
         wait_all(others, in_send.at[s, j, h])
 
     def hand(s, h, low, high):
-        @pl.loop(low, high)
-        def _(j):
-            vacant(s, j, h)
-            outgoing[s, span(h), piece(j)] = term(s, j, h).astype(jnp.bfloat16)
-            exchange(s, j, h, orecv, out_send, out_recv)
+        for first, end in ((low, min(high, ahead[s])), (max(low, ahead[s]), high)):
+            if first < end:
+
+                @pl.loop(first, end)
+                def _(j):
+                    if first >= ahead[s]:
+                        vacant(s, j, h)
+                    outgoing[s, span(h), piece(j)] = term(s, j, h).astype(jnp.bfloat16)
+                    exchange(s, j, h, orecv, out_send, out_recv)
 
     def hand_across(s, h):
         for j in range(astern[s]):
@@ -311,29 +315,27 @@
     for s in steps:
         weight_copy(1, s).wait()
         weight_copy(2, s).wait()
-    hand(0, 0, max(astern), pieces)
-    for s in range(1, nt):
-        hand_across(s, 0)
-    for s in [*range(1, early), *([last] if last >= early else [])]:
+    far = list(reversed(range(early, nt)))
+    near = list(reversed(range(1, early)))
+    for i, s in enumerate(far):
         hand(s, 0, astern[s], pieces)
+        if i == 0:
+            for q in range(1, nt):
+                hand_across(q, 0)
     for s in range(1, nt):
         contract(s, 1)
     activate(1)
-    for s in reversed(range(early, nt)):
-        if s < last:
-            hand(s, 0, astern[s], pieces)
+    for s in far:
         hand(s, 1, astern[s], pieces)
-        if s == last:
-            for q in range(1, nt):
-                hand_across(q, 1)
-    for s in reversed(range(1, early)):
-        hand(s, 1, astern[s], pieces)
-    send_back_own(0)
-    hand(0, 1, max(astern), pieces)
-    send_back_own(1)
-
-    for s in reversed(range(1, nt)):
-
+    for q in range(1, nt):
+        hand_across(q, 1)
+    for s in near:
+        for h in halves:
+            hand(s, h, astern[s], pieces)
+    for h in halves:
+        hand(0, h, max(astern), pieces)
+
+    def finish(s):
         @pl.loop(astern[s], pieces)
         def _(j):
             for h in halves:
@@ -341,6 +343,14 @@
             part[s, :, piece(j)] = combine(s, j).astype(jnp.bfloat16)
 
         p_copies[s].start()
+
+    for s in far:
+        finish(s)
+    for h in halves:
+        send_back_own(h)
+
+    for s in near:
+        finish(s)
     for s in range(1, nt):
         p_copies[s].wait_recv()
     for j in [*range(max(astern), pieces), *reversed(range(max(astern)))]:

time: 95.7 us -> 91.9 us (0.960)
  Pallas kernels: 93.9 us -> 90.1 us
    pallas_call x1, Pallas kernels: 93.9 us -> 90.1 us  [shards(): pl.pallas_call(functools.partial(kernel, ne, nt, cap), out_shape=jax.Shap...]
where the time goes in v3:
time: 91.9 us; the launch traced here: 91.8 us
  Pallas kernels  90.1 us (98%)
  local copies, waits for them, and re-layouts  1.67 us (2%)
    pallas_call x1, Pallas kernels, shards(): pl.pallas_call(functools.partial(kernel, ne, nt, cap), out_shape=jax.Shap...  90.1 us

profile of v3, /device:TPU:0, one launch (start us, length us, event | category | flops | bytes accessed | tf_op | source)
XLA Modules:
  0.0 91.8 jit_solution(16676907676539046619)
XLA Ops:
  0.0 90.1 %shard_map.82 = bf16[128,1024]{1,0:T(8,128)(2,1)} custom-call(bf16[128,1024]{1,0:T(8,128)(2,1)} %raw0.1, s32[4,128]{1,0:T(4,128)} %bitcast.3, f32[4,128]{1,0:T(4,128)} %bitcast.4, s32[1,128]{1,0:T(1,128)} %bitcast.5, bf16[1,1344,4096]{2,1,0:T(8,128)(2,1)} %w_gate.1, bf16[1,1344,4096]{2,1,0:T(8,128)(2,1)} %w_up.1, bf16[1,1344,4096]{2,1,0:T(8,128)(2,1)} %w_down.1, ...), custom_call_target="tpu_custom_call" | custom-call | tf_op jit(solution)/shard_map/pallas_call | solution.py:392
  90.1 1.7 %copy.10 = bf16[128,1024]{1,0:T(8,128)(2,1)} copy(bf16[128,1024]{1,0:T(8,128)(2,1)} %shard_map.82) | data formatting | bytes 524288
